TPU v7x, 512 devices: a whole 4x4x16 slice. The times are simulated.
512 devices in a mesh: shot: 16 (over z_lo, core), recv: 32 (over z_hi, y, x).
Axes of the slice: x: 4, y: 4, z: 16 (z_hi: 2, z_lo: 8; z = z_hi * 8 + z_lo), core: 2. Of those that a mesh axis runs over, the one named last changes fastest.
Arguments:
- pressure: bfloat16 [2, 6144, 6144], P(None, 'recv', 'shot'), may hold values from -6 to 6
Outputs:
- multiples: float32 [2, 6144, 6144], P(None, 'recv', 'shot')
All inputs are finite; a program needn't handle non-finite values.
Results may differ from a plain program's by a relative error of at most 0.0044.
Values may be sent and summed in bfloat16 or wider, within the bound.
No kernel may reach another device: no remote copies, remote signals or barrier semaphores. Data moves between devices by JAX's collectives and lax.ppermute only.
A program may use at most 64 MiB of HBM per device.

v0:
```python
import math
import jax
import jax.numpy as jnp
from jax import lax
from jax.sharding import PartitionSpec as P

N = 6144


def partner(value, axis, apart):
    mask = 2**apart
    pairs = [(source, source ^ mask) for source in range(lax.axis_size(axis))]
    return lax.ppermute(value, axis, pairs)


def local(pressure):
    block_rows = pressure.shape[1]
    block_cols = pressure.shape[2]
    shot_index = lax.axis_index("shot")
    recv_index = lax.axis_index("recv")
    grid_row = recv_index // 2
    pair_bit = recv_index % 2
    mirror = pressure
    levels = lax.axis_size("shot").bit_length() - 1
    for bit_index in range(levels):
        stride = 2**bit_index
        agrees = shot_index // stride % 2 == grid_row // stride % 2
        transit = partner(mirror, "shot", bit_index)
        arrived = partner(transit, "recv", bit_index + 1)
        mirror = jnp.where(agrees, mirror, arrived)
    kept_cols = lax.dynamic_slice_in_dim(mirror, pair_bit * block_rows, block_rows, 2)
    given_cols = lax.dynamic_slice_in_dim(mirror, (1 - pair_bit) * block_rows, block_rows, 2)
    taken_cols = partner(given_cols, "recv", 0)
    stacked = jnp.where(
        pair_bit == 0,
        jnp.concatenate([kept_cols, taken_cols], axis=1),
        jnp.concatenate([taken_cols, kept_cols], axis=1),
    )
    symmetric = (
        (pressure.astype(jnp.float32) + jnp.swapaxes(stacked, 1, 2).astype(jnp.float32)) * 0.5
    ).astype(jnp.bfloat16)
    factor = 1.0 / math.sqrt(N)
    row_panel = lax.all_gather(symmetric, "shot", axis=2, tiled=True)
    shard_block = lax.all_gather(symmetric, "recv", axis=1, tiled=True)
    left_real = row_panel[0]
    left_imag = row_panel[1]
    upper_half = jnp.concatenate([shard_block[0], shard_block[1]], axis=1)
    lower_half = jnp.concatenate([-shard_block[1], shard_block[0]], axis=1)
    running = jnp.dot(left_real, upper_half, preferred_element_type=jnp.float32)
    running = running + jnp.dot(left_imag, lower_half, preferred_element_type=jnp.float32)
    running = running * factor
    return jnp.stack([running[:, :block_cols], running[:, block_cols:]])


def solution(mesh):
    placed = (P(None, "recv", "shot"),)
    return jax.shard_map(
        local, mesh=mesh, in_specs=placed, out_specs=P(None, "recv", "shot"), check_vma=False
    )
```

profile of v0, /device:TPU:2, one launch (start us, length us, event | category | flops | bytes accessed | tf_op | source)
XLA Modules:
  0.0 570.4 jit_solution(5705940932931412052)
XLA Ops:
  6.5 0.0 copy-start.3
  6.5 0.0 all-gather.5.cloned.1.call-start
  6.5 1.2 copy.3
  7.7 1.9 collective-permute-start
  9.7 1.7 collective-permute-done
  11.4 4.0 collective-permute-start.1
  15.4 10.5 %collective-permute-done.1 = bf16[2,192,384]{1,2,0:T(8,128)(2,1)S(1)} collective-permute-done((bf16[2,192,384]{1,2,0:T(8,128)(2,1)S(1)}, bf16[2,192,384]{1,2,0:T(8,128)(2,1)S(1)}, u32[]{:S(2)}, u32[]{:S(2)}) %collective-permute-start.1) | collective-permute-done | bytes 294944 | tf_op jit(solution)/shard_map/ppermute | solution.py:13
  25.9 3.8 collective-permute-start.2
  29.8 8.6 %collective-permute-done.2 = bf16[2,192,384]{1,2,0:T(8,128)(2,1)S(1)} collective-permute-done((bf16[2,192,384]{1,2,0:T(8,128)(2,1)S(1)}, bf16[2,192,384]{1,2,0:T(8,128)(2,1)S(1)}, u32[]{:S(2)}, u32[]{:S(2)}) %collective-permute-start.2) | collective-permute-done | bytes 294944 | tf_op jit(solution)/shard_map/ppermute | solution.py:13
  38.4 3.5 collective-permute-start.3
  41.9 7.9 %collective-permute-done.3 = bf16[2,192,384]{1,2,0:T(8,128)(2,1)S(1)} collective-permute-done((bf16[2,192,384]{1,2,0:T(8,128)(2,1)S(1)}, bf16[2,192,384]{1,2,0:T(8,128)(2,1)S(1)}, u32[]{:S(2)}, u32[]{:S(2)}) %collective-permute-start.3) | collective-permute-done | bytes 294944 | tf_op jit(solution)/shard_map/ppermute | solution.py:13
  49.9 5.2 collective-permute-start.4
  55.1 15.3 %collective-permute-done.4 = bf16[2,192,384]{1,2,0:T(8,128)(2,1)S(1)} collective-permute-done((bf16[2,192,384]{1,2,0:T(8,128)(2,1)S(1)}, bf16[2,192,384]{1,2,0:T(8,128)(2,1)S(1)}, u32[]{:S(2)}, u32[]{:S(2)}) %collective-permute-start.4) | collective-permute-done | bytes 294944 | tf_op jit(solution)/shard_map/ppermute | solution.py:13
  70.4 5.1 collective-permute-start.5
  75.6 8.4 %collective-permute-done.5 = bf16[2,192,384]{1,2,0:T(8,128)(2,1)S(1)} collective-permute-done((bf16[2,192,384]{1,2,0:T(8,128)(2,1)S(1)}, bf16[2,192,384]{1,2,0:T(8,128)(2,1)S(1)}, u32[]{:S(2)}, u32[]{:S(2)}) %collective-permute-start.5) | collective-permute-done | bytes 294944 | tf_op jit(solution)/shard_map/ppermute | solution.py:13
  84.0 9.1 %collective-permute-start.6 = (bf16[2,192,384]{1,2,0:T(8,128)(2,1)S(1)}, bf16[2,192,384]{1,2,0:T(8,128)(2,1)S(1)}, u32[]{:S(2)}, u32[]{:S(2)}) collective-permute-start(bf16[2,192,384]{1,2,0:T(8,128)(2,1)S(1)} %broadcast_select_fusion.2), channel_id=1, source_target_pairs={{0,256},{32,288},{64,320},{96,352},{128,384},{160,416},{192,448},{... | collective-permute-start | bytes 884744 | tf_op jit(solution)/shard_map/ppermute | solution.py:13
  93.1 31.7 %collective-permute-done.6 = bf16[2,192,384]{1,2,0:T(8,128)(2,1)S(1)} collective-permute-done((bf16[2,192,384]{1,2,0:T(8,128)(2,1)S(1)}, bf16[2,192,384]{1,2,0:T(8,128)(2,1)S(1)}, u32[]{:S(2)}, u32[]{:S(2)}) %collective-permute-start.6) | collective-permute-done | bytes 294944 | tf_op jit(solution)/shard_map/ppermute | solution.py:13
  124.8 21.9 %collective-permute-start.7 = (bf16[2,192,384]{1,2,0:T(8,128)(2,1)S(1)}, bf16[2,192,384]{1,2,0:T(8,128)(2,1)S(1)}, u32[]{:S(2)}, u32[]{:S(2)}) collective-permute-start(bf16[2,192,384]{1,2,0:T(8,128)(2,1)S(1)} %collective-permute-done.6), channel_id=1, source_target_pairs={{0,16},{1,17},{2,18},{3,19},{4,20},{5,21},{6,22},{7,23},{8,24},{9,... | collective-permute-start | bytes 884744 | tf_op jit(solution)/shard_map/ppermute | solution.py:13
  146.8 14.6 %collective-permute-done.7 = bf16[2,192,384]{1,2,0:T(8,128)(2,1)S(1)} collective-permute-done((bf16[2,192,384]{1,2,0:T(8,128)(2,1)S(1)}, bf16[2,192,384]{1,2,0:T(8,128)(2,1)S(1)}, u32[]{:S(2)}, u32[]{:S(2)}) %collective-permute-start.7) | collective-permute-done | bytes 294944 | tf_op jit(solution)/shard_map/ppermute | solution.py:13
  161.4 2.4 collective-permute-start.8
  163.9 6.2 %collective-permute-done.8 = bf16[2,192,192]{1,2,0:T(8,128)(2,1)S(1)} collective-permute-done((bf16[2,192,192]{1,2,0:T(8,128)(2,1)S(1)}, bf16[2,192,192]{1,2,0:T(8,128)(2,1)S(1)}, u32[]{:S(2)}, u32[]{:S(2)}) %collective-permute-start.8) | collective-permute-done | bytes 147488 | tf_op jit(solution)/shard_map/ppermute | solution.py:13
  170.1 0.0 copy-done.3
  170.1 1.0 fusion.15
  171.1 0.0 all-gather.5.cloned.1.call-update
  171.1 0.0 all-gather.3.cloned.1.call-start
  171.2 0.7 all-gather.3.cloned.1.call-update
  171.9 269.1 %all-gather.5.cloned.1.call-done = bf16[2,6144,384]{2,1,0:T(8,128)(2,1)} async-done(((bf16[2,192,384]{2,1,0:T(8,128)(2,1)}), bf16[2,6144,384]{2,1,0:T(8,128)(2,1)}) %all-gather.5.cloned.1.call-update) | async-done | bytes 9437200 | tf_op jit(solution)/shard_map/all_gather | solution.py:44
  440.9 0.0 copy-start
  440.9 5.3 fusion.18
  446.2 1.5 copy-done
  447.7 4.6 slice_bitcast_fusion.1
  452.4 99.8 %all-gather.3.cloned.1.call-done = bf16[2,192,6144]{2,1,0:T(8,128)(2,1)} async-done(((bf16[2,192,384]{2,1,0:T(8,128)(2,1)}), bf16[2,192,6144]{2,1,0:T(8,128)(2,1)}) %all-gather.3.cloned.1.call-update) | async-done | bytes 4718608 | tf_op jit(solution)/shard_map/all_gather | solution.py:43
  552.1 0.0 copy-start.1
  552.1 0.0 copy-start.2
  552.1 0.0 copy-start.4
  552.1 6.5 %fusion = f32[192,768]{1,0:T(8,128)S(1)} fusion(bf16[6144,384]{1,0:T(8,128)(2,1)} %get-tuple-element.6, bf16[6144,384]{1,0:T(8,128)(2,1)} %get-tuple-element.5, bf16[2,192,6144]{2,1,0:T(8,128)(2,1)} %all-gather.3.cloned.1.call-done), kind=kOutput, calls=%fused_computation | convolution fusion | flops 1830813696 | bytes 12386304 | tf_op jit(solution)/shard_map/dot_general | solution.py:49
  558.7 0.0 copy-done.1
  558.7 0.6 copy-done.2
  559.3 1.3 copy-done.4
  560.7 2.0 fusion.11
  562.7 0.9 pad_maximum_fusion
  (6 shorter events, 0.2 us)
Async XLA Ops:
  6.5 163.6 %copy-start.3 = (bf16[2,192,384]{2,1,0:T(8,128)(2,1)S(1)}, bf16[2,192,384]{2,1,0:T(8,128)(2,1)}, u32[]{:S(2)}) copy-start(bf16[2,192,384]{2,1,0:T(8,128)(2,1)} %param.1) | copy-start | bytes 884740
  6.5 434.4 %all-gather.5.cloned.1.call-start = ((), (), s32[]{:S(2)}) async-start(), calls=%async_computation.1 | async-start | bytes 9732096 | tf_op jit(solution)/shard_map/all_gather | solution.py:44
  7.7 3.6 collective-permute-start
  11.4 14.5 %collective-permute-start.1 = (bf16[2,192,384]{1,2,0:T(8,128)(2,1)S(1)}, bf16[2,192,384]{1,2,0:T(8,128)(2,1)S(1)}, u32[]{:S(2)}, u32[]{:S(2)}) collective-permute-start(bf16[2,192,384]{1,2,0:T(8,128)(2,1)S(1)} %collective-permute-done), channel_id=1, source_target_pairs={{0,2},{1,3},{2,0},{3,1},{4,6},{5,7},{6,4},{7,5},{8,10},{9,11},{10,... | collective-permute-start | bytes 884744 | tf_op jit(solution)/shard_map/ppermute | solution.py:13
  25.9 12.4 %collective-permute-start.2 = (bf16[2,192,384]{1,2,0:T(8,128)(2,1)S(1)}, bf16[2,192,384]{1,2,0:T(8,128)(2,1)S(1)}, u32[]{:S(2)}, u32[]{:S(2)}) collective-permute-start(bf16[2,192,384]{1,2,0:T(8,128)(2,1)S(1)} %broadcast_select_fusion), channel_id=1, source_target_pairs={{0,64},{32,96},{64,0},{96,32},{128,192},{160,224},{192,128},{224,1... | collective-permute-start | bytes 884744 | tf_op jit(solution)/shard_map/ppermute | solution.py:13
  38.4 11.5 %collective-permute-start.3 = (bf16[2,192,384]{1,2,0:T(8,128)(2,1)S(1)}, bf16[2,192,384]{1,2,0:T(8,128)(2,1)S(1)}, u32[]{:S(2)}, u32[]{:S(2)}) collective-permute-start(bf16[2,192,384]{1,2,0:T(8,128)(2,1)S(1)} %collective-permute-done.2), channel_id=1, source_target_pairs={{0,4},{1,5},{2,6},{3,7},{4,0},{5,1},{6,2},{7,3},{8,12},{9,13},{10,... | collective-permute-start | bytes 884744 | tf_op jit(solution)/shard_map/ppermute | solution.py:13
  49.9 20.5 %collective-permute-start.4 = (bf16[2,192,384]{1,2,0:T(8,128)(2,1)S(1)}, bf16[2,192,384]{1,2,0:T(8,128)(2,1)S(1)}, u32[]{:S(2)}, u32[]{:S(2)}) collective-permute-start(bf16[2,192,384]{1,2,0:T(8,128)(2,1)S(1)} %broadcast_select_fusion.1), channel_id=1, source_target_pairs={{0,128},{32,160},{64,192},{96,224},{128,0},{160,32},{192,64},{224,... | collective-permute-start | bytes 884744 | tf_op jit(solution)/shard_map/ppermute | solution.py:13
  70.4 13.5 %collective-permute-start.5 = (bf16[2,192,384]{1,2,0:T(8,128)(2,1)S(1)}, bf16[2,192,384]{1,2,0:T(8,128)(2,1)S(1)}, u32[]{:S(2)}, u32[]{:S(2)}) collective-permute-start(bf16[2,192,384]{1,2,0:T(8,128)(2,1)S(1)} %collective-permute-done.4), channel_id=1, source_target_pairs={{0,8},{1,9},{2,10},{3,11},{4,12},{5,13},{6,14},{7,15},{8,0},{9,1},... | collective-permute-start | bytes 884744 | tf_op jit(solution)/shard_map/ppermute | solution.py:13
  84.0 40.8 %collective-permute-start.6 = (bf16[2,192,384]{1,2,0:T(8,128)(2,1)S(1)}, bf16[2,192,384]{1,2,0:T(8,128)(2,1)S(1)}, u32[]{:S(2)}, u32[]{:S(2)}) collective-permute-start(bf16[2,192,384]{1,2,0:T(8,128)(2,1)S(1)} %broadcast_select_fusion.2), channel_id=1, source_target_pairs={{0,256},{32,288},{64,320},{96,352},{128,384},{160,416},{192,448},{... | collective-permute-start | bytes 884744 | tf_op jit(solution)/shard_map/ppermute | solution.py:13
  124.8 36.5 %collective-permute-start.7 = (bf16[2,192,384]{1,2,0:T(8,128)(2,1)S(1)}, bf16[2,192,384]{1,2,0:T(8,128)(2,1)S(1)}, u32[]{:S(2)}, u32[]{:S(2)}) collective-permute-start(bf16[2,192,384]{1,2,0:T(8,128)(2,1)S(1)} %collective-permute-done.6), channel_id=1, source_target_pairs={{0,16},{1,17},{2,18},{3,19},{4,20},{5,21},{6,22},{7,23},{8,24},{9,... | collective-permute-start | bytes 884744 | tf_op jit(solution)/shard_map/ppermute | solution.py:13
  161.4 8.6 %collective-permute-start.8 = (bf16[2,192,192]{1,2,0:T(8,128)(2,1)S(1)}, bf16[2,192,192]{1,2,0:T(8,128)(2,1)S(1)}, u32[]{:S(2)}, u32[]{:S(2)}) collective-permute-start(bf16[2,192,192]{1,2,0:T(8,128)(2,1)S(1)} %get-tuple-element.10), channel_id=1, source_target_pairs={{0,1},{1,0},{2,3},{3,2},{4,5},{5,4},{6,7},{7,6},{8,9},{9,8},{10,11... | collective-permute-start | bytes 442376 | tf_op jit(solution)/shard_map/ppermute | solution.py:13
  171.1 381.0 %all-gather.3.cloned.1.call-start = ((), (), s32[]{:S(2)}) async-start(), calls=%async_computation | async-start | bytes 5013504 | tf_op jit(solution)/shard_map/all_gather | solution.py:43
  440.9 6.8 %copy-start = (bf16[2,6144,384]{2,1,0:T(8,128)(2,1)S(1)}, bf16[2,6144,384]{2,1,0:T(8,128)(2,1)}, u32[]{:S(2)}) copy-start(bf16[2,6144,384]{2,1,0:T(8,128)(2,1)} %all-gather.5.cloned.1.call-done) | copy-start | bytes 28311556
  552.1 6.5 %copy-start.1 = (bf16[6144,384]{1,0:T(8,128)(2,1)S(1)}, bf16[6144,384]{1,0:T(8,128)(2,1)}, u32[]{:S(2)}) copy-start(bf16[6144,384]{1,0:T(8,128)(2,1)} %fusion.18) | copy-start | bytes 14155780
  552.1 7.2 %copy-start.2 = (bf16[6144,384]{1,0:T(8,128)(2,1)S(1)}, bf16[6144,384]{1,0:T(8,128)(2,1)}, u32[]{:S(2)}) copy-start(bf16[6144,384]{1,0:T(8,128)(2,1)} %get-tuple-element.5) | copy-start | bytes 14155780
  552.1 8.5 %copy-start.4 = (bf16[2,192,6144]{2,1,0:T(8,128)(2,1)S(1)}, bf16[2,192,6144]{2,1,0:T(8,128)(2,1)}, u32[]{:S(2)}) copy-start(bf16[2,192,6144]{2,1,0:T(8,128)(2,1)} %all-gather.3.cloned.1.call-done) | copy-start | bytes 14155780
Sparse Core Ops, SparseCore 0:
  171.2 269.6 all-gather.4
  443.0 109.0 all-gather.2
where the time goes:
time: 571 us; the launch traced here: 570 us
  waiting for transfers between devices  474 us (83%)
  starting transfers between devices  57 us (10%)
  between operations  13.8 us (2%)
  local copies, waits for them, and re-layouts  9.36 us (2%)
  matrix products  8.52 us (1%)
  other arithmetic  7.32 us (1%)
    all_gather x1, waiting for transfers between devices, local(): shard_block = lax.all_gather(symmetric, 'recv', axis=1, tiled=True)  269 us
    ppermute x9, waiting for transfers between devices, partner(): return lax.ppermute(value, axis, pairs)  105 us
    all_gather x1, waiting for transfers between devices, local(): row_panel = lax.all_gather(symmetric, 'shot', axis=2, tiled=True)  99.8 us
    ppermute x9, starting transfers between devices, partner(): return lax.ppermute(value, axis, pairs)  56.9 us
  transfers between devices with their start and end apart: 11, of which 11 were waited for; matrix products, arithmetic and copies ran while one was open for 2% of the time, Pallas kernels for 0%

commit v1 on v0

--- a/solution.py
+++ b/solution.py
@@ -41,7 +41,9 @@
     ).astype(jnp.bfloat16)
     factor = 1.0 / math.sqrt(N)
     row_panel = lax.all_gather(symmetric, "shot", axis=2, tiled=True)
-    shard_block = lax.all_gather(symmetric, "recv", axis=1, tiled=True)
+    shard_block = jnp.concatenate(
+        lax.all_to_all(jnp.stack([symmetric] * lax.axis_size("recv")), "recv", 0, 0), axis=1
+    )
     left_real = row_panel[0]
     left_imag = row_panel[1]
     upper_half = jnp.concatenate([shard_block[0], shard_block[1]], axis=1)

time: 571 us -> 709 us (1.24)
  the two profiles are of different devices: /device:TPU:2 before, /device:TPU:469 now
where the time goes in v1:
time: 709 us
  waiting for transfers between devices  623 us (88%)
  starting transfers between devices  41.8 us (6%)
  local copies, waits for them, and re-layouts  17.3 us (2%)
  between operations  13.8 us (2%)
  matrix products  8.52 us (1%)
    all_to_all x1, waiting for transfers between devices, local(): lax.all_to_all(jnp.stack([symmetric] * lax.axis_size('recv')), 'recv', 0, 0)  506 us
    ppermute x9, waiting for transfers between devices, partner(): return lax.ppermute(value, axis, pairs)  116 us
    ppermute x9, starting transfers between devices, partner(): return lax.ppermute(value, axis, pairs)  25.2 us
    all_to_all x1, starting transfers between devices, local(): lax.all_to_all(jnp.stack([symmetric] * lax.axis_size('recv')), 'recv', 0, 0)  16.5 us
  transfers between devices with their start and end apart: 11, of which 10 were waited for; matrix products, arithmetic and copies ran while one was open for 1% of the time, Pallas kernels for 0%

profile of v1, /device:TPU:469, one launch (start us, length us, event | category | flops | bytes accessed | tf_op | source)
XLA Modules:
  0.0 708.5 jit_solution(13855503193652914772)
XLA Ops:
  6.5 0.0 copy-start.3
  6.5 1.2 copy.3
  7.7 2.6 collective-permute-start
  10.3 1.3 collective-permute-done
  11.7 2.1 collective-permute-start.1
  13.8 11.5 %collective-permute-done.1 = bf16[2,192,384]{1,2,0:T(8,128)(2,1)S(1)} collective-permute-done((bf16[2,192,384]{1,2,0:T(8,128)(2,1)S(1)}, bf16[2,192,384]{1,2,0:T(8,128)(2,1)S(1)}, u32[]{:S(2)}, u32[]{:S(2)}) %collective-permute-start.1) | collective-permute-done | bytes 294944 | tf_op jit(solution)/shard_map/ppermute | solution.py:13
  25.4 2.6 collective-permute-start.2
  28.1 8.6 %collective-permute-done.2 = bf16[2,192,384]{1,2,0:T(8,128)(2,1)S(1)} collective-permute-done((bf16[2,192,384]{1,2,0:T(8,128)(2,1)S(1)}, bf16[2,192,384]{1,2,0:T(8,128)(2,1)S(1)}, u32[]{:S(2)}, u32[]{:S(2)}) %collective-permute-start.2) | collective-permute-done | bytes 294944 | tf_op jit(solution)/shard_map/ppermute | solution.py:13
  36.7 2.9 collective-permute-start.3
  39.7 7.4 %collective-permute-done.3 = bf16[2,192,384]{1,2,0:T(8,128)(2,1)S(1)} collective-permute-done((bf16[2,192,384]{1,2,0:T(8,128)(2,1)S(1)}, bf16[2,192,384]{1,2,0:T(8,128)(2,1)S(1)}, u32[]{:S(2)}, u32[]{:S(2)}) %collective-permute-start.3) | collective-permute-done | bytes 294944 | tf_op jit(solution)/shard_map/ppermute | solution.py:13
  47.1 3.1 collective-permute-start.4
  50.2 16.7 %collective-permute-done.4 = bf16[2,192,384]{1,2,0:T(8,128)(2,1)S(1)} collective-permute-done((bf16[2,192,384]{1,2,0:T(8,128)(2,1)S(1)}, bf16[2,192,384]{1,2,0:T(8,128)(2,1)S(1)}, u32[]{:S(2)}, u32[]{:S(2)}) %collective-permute-start.4) | collective-permute-done | bytes 294944 | tf_op jit(solution)/shard_map/ppermute | solution.py:13
  66.9 2.0 collective-permute-start.5
  69.0 11.0 %collective-permute-done.5 = bf16[2,192,384]{1,2,0:T(8,128)(2,1)S(1)} collective-permute-done((bf16[2,192,384]{1,2,0:T(8,128)(2,1)S(1)}, bf16[2,192,384]{1,2,0:T(8,128)(2,1)S(1)}, u32[]{:S(2)}, u32[]{:S(2)}) %collective-permute-start.5) | collective-permute-done | bytes 294944 | tf_op jit(solution)/shard_map/ppermute | solution.py:13
  80.0 5.2 collective-permute-start.6
  85.2 28.0 %collective-permute-done.6 = bf16[2,192,384]{1,2,0:T(8,128)(2,1)S(1)} collective-permute-done((bf16[2,192,384]{1,2,0:T(8,128)(2,1)S(1)}, bf16[2,192,384]{1,2,0:T(8,128)(2,1)S(1)}, u32[]{:S(2)}, u32[]{:S(2)}) %collective-permute-start.6) | collective-permute-done | bytes 294944 | tf_op jit(solution)/shard_map/ppermute | solution.py:13
  113.1 1.9 collective-permute-start.7
  115.2 27.1 %collective-permute-done.7 = bf16[2,192,384]{1,2,0:T(8,128)(2,1)S(1)} collective-permute-done((bf16[2,192,384]{1,2,0:T(8,128)(2,1)S(1)}, bf16[2,192,384]{1,2,0:T(8,128)(2,1)S(1)}, u32[]{:S(2)}, u32[]{:S(2)}) %collective-permute-start.7) | collective-permute-done | bytes 294944 | tf_op jit(solution)/shard_map/ppermute | solution.py:13
  142.3 2.8 collective-permute-start.8
  145.1 4.7 collective-permute-done.8
  149.9 0.0 copy-done.3
  149.9 0.3 fusion.15
  150.2 0.0 copy-start.2
  150.2 5.2 stack.8
  155.3 0.0 copy-done.2
  155.3 16.5 %all-to-all-start = ((bf16[32,2,192,384]{3,2,1,0:T(8,128)(2,1)}), bf16[32,2,192,384]{3,2,1,0:T(8,128)(2,1)}, u32[]{:S(2)}, u32[]{:S(2)}) async-start(bf16[32,2,192,384]{3,2,1,0:T(8,128)(2,1)} %stack.8), calls=%async_computation | async-start | bytes 18874368 | tf_op jit(solution)/shard_map/all_to_all | solution.py:45
  171.9 0.0 all-gather.2.cloned.1.call-start
  171.9 0.7 all-gather.2.cloned.1.call-update
  172.6 505.7 %all-to-all-done = bf16[32,2,192,384]{3,2,1,0:T(8,128)(2,1)} async-done(((bf16[32,2,192,384]{3,2,1,0:T(8,128)(2,1)}), bf16[32,2,192,384]{3,2,1,0:T(8,128)(2,1)}, u32[]{:S(2)}, u32[]{:S(2)}) %all-to-all-start) | async-done | bytes 9437216 | tf_op jit(solution)/shard_map/all_to_all | solution.py:45
  678.3 7.0 fusion.18
  685.2 0.0 copy-start
  685.3 2.1 copy-done
  687.4 0.0 slice-start
  687.4 3.0 bitcast_negate_fusion
  690.4 0.0 all-gather.2.cloned.1.call-done
  690.4 0.0 copy-start.1
  690.4 0.0 slice-start.1
  690.4 0.0 copy-start.4
  690.4 6.5 fusion
  697.0 0.0 slice-done
  697.0 0.0 copy-done.1
  697.0 0.5 slice-done.1
  697.4 1.3 copy-done.4
  698.8 2.0 fusion.11
  700.8 0.9 pad_maximum_fusion
  (7 shorter events, 0.2 us)
Async XLA Ops:
  6.5 143.3 %copy-start.3 = (bf16[2,192,384]{2,1,0:T(8,128)(2,1)S(1)}, bf16[2,192,384]{2,1,0:T(8,128)(2,1)}, u32[]{:S(2)}) copy-start(bf16[2,192,384]{2,1,0:T(8,128)(2,1)} %param.1) | copy-start | bytes 884740
  7.7 3.9 collective-permute-start
  11.7 13.7 %collective-permute-start.1 = (bf16[2,192,384]{1,2,0:T(8,128)(2,1)S(1)}, bf16[2,192,384]{1,2,0:T(8,128)(2,1)S(1)}, u32[]{:S(2)}, u32[]{:S(2)}) collective-permute-start(bf16[2,192,384]{1,2,0:T(8,128)(2,1)S(1)} %collective-permute-done), channel_id=1, source_target_pairs={{0,2},{1,3},{2,0},{3,1},{4,6},{5,7},{6,4},{7,5},{8,10},{9,11},{10,... | collective-permute-start | bytes 884744 | tf_op jit(solution)/shard_map/ppermute | solution.py:13
  25.4 11.3 %collective-permute-start.2 = (bf16[2,192,384]{1,2,0:T(8,128)(2,1)S(1)}, bf16[2,192,384]{1,2,0:T(8,128)(2,1)S(1)}, u32[]{:S(2)}, u32[]{:S(2)}) collective-permute-start(bf16[2,192,384]{1,2,0:T(8,128)(2,1)S(1)} %broadcast_select_fusion), channel_id=1, source_target_pairs={{0,64},{32,96},{64,0},{96,32},{128,192},{160,224},{192,128},{224,1... | collective-permute-start | bytes 884744 | tf_op jit(solution)/shard_map/ppermute | solution.py:13
  36.7 10.4 %collective-permute-start.3 = (bf16[2,192,384]{1,2,0:T(8,128)(2,1)S(1)}, bf16[2,192,384]{1,2,0:T(8,128)(2,1)S(1)}, u32[]{:S(2)}, u32[]{:S(2)}) collective-permute-start(bf16[2,192,384]{1,2,0:T(8,128)(2,1)S(1)} %collective-permute-done.2), channel_id=1, source_target_pairs={{0,4},{1,5},{2,6},{3,7},{4,0},{5,1},{6,2},{7,3},{8,12},{9,13},{10,... | collective-permute-start | bytes 884744 | tf_op jit(solution)/shard_map/ppermute | solution.py:13
  47.1 19.8 %collective-permute-start.4 = (bf16[2,192,384]{1,2,0:T(8,128)(2,1)S(1)}, bf16[2,192,384]{1,2,0:T(8,128)(2,1)S(1)}, u32[]{:S(2)}, u32[]{:S(2)}) collective-permute-start(bf16[2,192,384]{1,2,0:T(8,128)(2,1)S(1)} %broadcast_select_fusion.1), channel_id=1, source_target_pairs={{0,128},{32,160},{64,192},{96,224},{128,0},{160,32},{192,64},{224,... | collective-permute-start | bytes 884744 | tf_op jit(solution)/shard_map/ppermute | solution.py:13
  66.9 13.0 %collective-permute-start.5 = (bf16[2,192,384]{1,2,0:T(8,128)(2,1)S(1)}, bf16[2,192,384]{1,2,0:T(8,128)(2,1)S(1)}, u32[]{:S(2)}, u32[]{:S(2)}) collective-permute-start(bf16[2,192,384]{1,2,0:T(8,128)(2,1)S(1)} %collective-permute-done.4), channel_id=1, source_target_pairs={{0,8},{1,9},{2,10},{3,11},{4,12},{5,13},{6,14},{7,15},{8,0},{9,1},... | collective-permute-start | bytes 884744 | tf_op jit(solution)/shard_map/ppermute | solution.py:13
  80.0 33.2 %collective-permute-start.6 = (bf16[2,192,384]{1,2,0:T(8,128)(2,1)S(1)}, bf16[2,192,384]{1,2,0:T(8,128)(2,1)S(1)}, u32[]{:S(2)}, u32[]{:S(2)}) collective-permute-start(bf16[2,192,384]{1,2,0:T(8,128)(2,1)S(1)} %broadcast_select_fusion.2), channel_id=1, source_target_pairs={{0,256},{32,288},{64,320},{96,352},{128,384},{160,416},{192,448},{... | collective-permute-start | bytes 884744 | tf_op jit(solution)/shard_map/ppermute | solution.py:13
  113.1 29.1 %collective-permute-start.7 = (bf16[2,192,384]{1,2,0:T(8,128)(2,1)S(1)}, bf16[2,192,384]{1,2,0:T(8,128)(2,1)S(1)}, u32[]{:S(2)}, u32[]{:S(2)}) collective-permute-start(bf16[2,192,384]{1,2,0:T(8,128)(2,1)S(1)} %collective-permute-done.6), channel_id=1, source_target_pairs={{0,16},{1,17},{2,18},{3,19},{4,20},{5,21},{6,22},{7,23},{8,24},{9,... | collective-permute-start | bytes 884744 | tf_op jit(solution)/shard_map/ppermute | solution.py:13
  142.3 7.6 %collective-permute-start.8 = (bf16[2,192,192]{1,2,0:T(8,128)(2,1)S(1)}, bf16[2,192,192]{1,2,0:T(8,128)(2,1)S(1)}, u32[]{:S(2)}, u32[]{:S(2)}) collective-permute-start(bf16[2,192,192]{1,2,0:T(8,128)(2,1)S(1)} %get-tuple-element.10), channel_id=1, source_target_pairs={{0,1},{1,0},{2,3},{3,2},{4,5},{5,4},{6,7},{7,6},{8,9},{9,8},{10,11... | collective-permute-start | bytes 442376 | tf_op jit(solution)/shard_map/ppermute | solution.py:13
  150.2 5.2 copy-start.2
  155.3 523.0 %all-to-all-start = ((bf16[32,2,192,384]{3,2,1,0:T(8,128)(2,1)}), bf16[32,2,192,384]{3,2,1,0:T(8,128)(2,1)}, u32[]{:S(2)}, u32[]{:S(2)}) async-start(bf16[32,2,192,384]{3,2,1,0:T(8,128)(2,1)} %stack.8), calls=%async_computation | async-start | bytes 18874368 | tf_op jit(solution)/shard_map/all_to_all | solution.py:45
  171.9 518.5 %all-gather.2.cloned.1.call-start = ((), (), s32[]{:S(2)}) async-start(), calls=%async_computation.1 | async-start | bytes 5013504 | tf_op jit(solution)/shard_map/all_gather | solution.py:43
  685.2 2.1 copy-start
  687.4 9.6 %slice-start = ((s8[4718592]{0:T(1024)(128)(4,1)}), s8[524288]{0:T(1024)(128)(4,1)S(1)}, s32[]{:S(2)}) async-start(s8[4718592]{0:T(1024)(128)(4,1)} %bitcast.26), calls=%async_computation.2 | async-start | bytes 1048576
  690.4 6.6 copy-start.1
  690.4 7.0 slice-start.1
  690.4 8.4 %copy-start.4 = (bf16[2,192,6144]{2,1,0:T(8,128)(2,1)S(1)}, bf16[2,192,6144]{2,1,0:T(8,128)(2,1)}, u32[]{:S(2)}) copy-start(bf16[2,192,6144]{2,1,0:T(8,128)(2,1)} %all-gather.2.cloned.1.call-done) | copy-start | bytes 14155780
Sparse Core Ops, SparseCore 0:
  174.8 406.7 all-gather.1
